TPU v7x, 128 devices: a whole 4x4x4 slice. The times are simulated.
128 devices in a mesh: seq: 32 (over x, z, core), tp: 4 (over y).
Axes of the slice: x: 4, y: 4, z: 4, core: 2. Of those that a mesh axis runs over, the one named last changes fastest.
Arguments:
- hidden: bfloat16 [4096, 2560], P('seq'), may hold values from -6 to 6
- gain_attn: float32 [2560], replicated, may hold values from 0.5 to 1.5
- w_query: bfloat16 [2560, 2560], P(None, 'tp')
- w_key: bfloat16 [2560, 512], P(None, 'tp'), as said below
- w_value: bfloat16 [2560, 512], P(None, 'tp'), may hold values from -0.125 to 0.125
- w_out: bfloat16 [2560, 2560], P('tp'), may hold values from -0.125 to 0.125
- gain_moe: float32 [2560], replicated, may hold values from 0.5 to 1.5
- expert_ids: int32 [4096, 6], P('seq'), may hold values from 0 to 63, all different within a row; in each aligned block of 128 rows (0 to 127, 128 to 255, ...) at most 24 rows name the same one
- expert_gates: float32 [4096, 6], P('seq'), may hold values from 0.05 to 0.3
- w_gate: bfloat16 [64, 2560, 1536], P('seq', None, 'tp'), may hold values from -0.125 to 0.125
- w_up: bfloat16 [64, 2560, 1536], P('seq', None, 'tp'), may hold values from -0.125 to 0.125
- w_down: bfloat16 [64, 1536, 2560], P('seq', 'tp'), may hold values from -0.15625 to 0.15625
- seg_lengths: int32 [16], replicated, may hold values from 1 to 1024, 4096 in all
- slot_page: int32 [2048], replicated, may hold values from -1 to 255, as said below
Outputs:
- hidden_out: bfloat16 [4096, 2560], P('seq', 'tp')
- kv_cache: bfloat16 [2048, 16, 1024], P('seq', None, 'tp')
Inputs may be any that keep to these rules, and one draw needn't show every extreme that they name: `expert_ids`: a row names 6 different experts; within the 128 rows of one index of seq no expert is named by more than 24 rows. `seg_lengths`: segment lengths in order, summing to 4096. `slot_page`: owner o holds slots o * 64 to o * 64 + 63 as 2 requests of 32 slots; a request lists 1 to 32 consecutive pages (after the last page comes page 0), then -1 in its remaining slots. `w_key`: key projection of fan-in scale.
All inputs are finite; a program needn't handle non-finite values.
Results may differ from a plain program's by a relative error of at most 0.015.
Values may be sent and summed in bfloat16 or wider, within the bound.
A program may use at most 192 MiB of HBM per device.

v0:
```python
import math
import jax
import jax.numpy as jnp
from jax import lax
from jax.sharding import PartitionSpec as P

HEAD_DIM = 128
TOP = 6
PAGE = 16
epsilon = 1e-05
rope_base = 500000.0
masked_score = -1e30


def rms_norm(values, gain_vec):
    widened = values.astype(jnp.float32)
    factor = lax.rsqrt(jnp.mean(widened * widened, axis=-1, keepdims=True) + epsilon)
    return (widened * factor * gain_vec).astype(jnp.bfloat16)


def rotate(values, position):
    half_dim = values.shape[-1] // 2
    inverse = rope_base ** (-2.0 * jnp.arange(half_dim, dtype=jnp.float32) / values.shape[-1])
    angles = position.astype(jnp.float32)[:, None] * inverse[None, :]
    cosine = jnp.cos(angles)[:, None, :]
    sine_part = jnp.sin(angles)[:, None, :]
    first_half = values[..., :half_dim]
    second_half = values[..., half_dim:]
    return jnp.concatenate(
        [
            first_half * cosine - second_half * sine_part,
            second_half * cosine + first_half * sine_part,
        ],
        axis=-1,
    )


def segment_start(seg_lengths, positions):
    bounds = jnp.cumsum(seg_lengths)
    starts = bounds - seg_lengths
    return jnp.max(jnp.where(starts[None, :] <= positions[:, None], starts[None, :], 0), axis=1)


def over_blocks(step_fn, carried, portion, key_positions):
    rows = portion.shape[0]
    size = math.gcd(rows, 512)
    count = rows // size
    stacked = portion.reshape((count, size) + portion.shape[1:])
    pos_stack = key_positions.reshape(count, size)

    def turn(state, item):
        return (step_fn(state, item[0], item[1]), None)

    carried, unused = lax.scan(turn, carried, (stacked, pos_stack))
    return carried


def attend_piece(
    soft_state,
    queries,
    piece_keys,
    piece_values,
    key_positions,
    query_positions,
    query_first,
    scaling,
):
    running_max, row_total, accum_sum = soft_state
    scores = (
        jnp.einsum("qkgd,skd->qkgs", queries, piece_keys, preferred_element_type=jnp.float32)
        * scaling
    )
    allowed = (key_positions[None, :] <= query_positions[:, None]) & (
        key_positions[None, :] >= query_first[:, None]
    )
    allowed = allowed[:, None, None, :]
    scores = jnp.where(allowed, scores, masked_score)
    new_max = jnp.maximum(running_max, jnp.max(scores, axis=-1))
    weights = jnp.where(allowed, jnp.exp(scores - new_max[..., None]), 0.0)
    rescale = jnp.exp(running_max - new_max)
    row_total = row_total * rescale + jnp.sum(weights, axis=-1)
    product = jnp.einsum(
        "qkgs,skd->qkgd",
        weights.astype(jnp.bfloat16),
        piece_values,
        preferred_element_type=jnp.float32,
    )
    accum_sum = accum_sum * rescale[..., None] + product
    return (new_max, row_total, accum_sum)


def local(
    hidden,
    gain_attn,
    w_query,
    w_key,
    w_value,
    w_out,
    gain_moe,
    expert_ids,
    expert_gates,
    w_gate,
    w_up,
    w_down,
    seg_lengths,
    slot_page,
):
    tok_rows = hidden.shape[0]
    model_width = hidden.shape[1]
    shard_count = lax.axis_size("seq")
    shard_index = lax.axis_index("seq")
    tensor_index = lax.axis_index("tp")
    quarter = model_width // lax.axis_size("tp")
    kv_local = w_key.shape[1] // HEAD_DIM
    q_local = w_query.shape[1] // HEAD_DIM
    group_size = q_local // kv_local
    positions = shard_index * tok_rows + jnp.arange(tok_rows, dtype=jnp.int32)
    seg_first = segment_start(seg_lengths, positions)
    offsets = positions - seg_first
    normed = rms_norm(hidden, gain_attn)
    query_raw = jnp.dot(normed, w_query, preferred_element_type=jnp.float32).reshape(
        tok_rows, q_local, HEAD_DIM
    )
    queries = (
        rotate(query_raw, offsets)
        .astype(jnp.bfloat16)
        .reshape(tok_rows, kv_local, group_size, HEAD_DIM)
    )
    key_raw = jnp.dot(normed, w_key, preferred_element_type=jnp.float32).reshape(
        tok_rows, kv_local, HEAD_DIM
    )
    keys_rot = rotate(key_raw, offsets).astype(jnp.bfloat16)
    values = (
        jnp.dot(normed, w_value, preferred_element_type=jnp.float32)
        .astype(jnp.bfloat16)
        .reshape(tok_rows, kv_local, HEAD_DIM)
    )
    kv_rows = jnp.stack([keys_rot, values], axis=2)
    row_width = 2 * kv_local * HEAD_DIM
    slot_count = slot_page.shape[0] // shard_count
    own_slots = lax.dynamic_slice_in_dim(slot_page, shard_index * slot_count, slot_count)
    wanted = own_slots[:, None, None] * PAGE + jnp.arange(PAGE, dtype=jnp.int32)[None, :, None]
    scaling = HEAD_DIM ** (-0.5)
    empty_max = jnp.full((tok_rows, kv_local, group_size), masked_score, jnp.float32)
    empty_total = jnp.zeros((tok_rows, kv_local, group_size), jnp.float32)
    empty_sum = jnp.zeros((tok_rows, kv_local, group_size, HEAD_DIM), jnp.float32)
    empty_cache = jnp.zeros((slot_count, PAGE, row_width), jnp.float32)

    def cache_rows(cache_acc, portion, key_positions):
        piece_rows = portion.shape[0]
        chosen = (wanted == key_positions[None, None, :]).astype(jnp.bfloat16)
        return cache_acc + jnp.einsum(
            "spc,cw->spw",
            chosen,
            portion.reshape(piece_rows, row_width),
            preferred_element_type=jnp.float32,
        )

    def attend_rows(soft_state, portion, key_positions):
        return attend_piece(
            soft_state,
            queries,
            portion[:, :, 0],
            portion[:, :, 1],
            key_positions,
            positions,
            seg_first,
            scaling,
        )

    def both_rows(carried, portion, key_positions):
        soft_state, cache_acc = carried
        return (
            attend_rows(soft_state, portion, key_positions),
            cache_rows(cache_acc, portion, key_positions),
        )

    portion = lax.all_gather(kv_rows, "seq", axis=0, tiled=True)
    key_positions = jnp.arange(portion.shape[0], dtype=jnp.int32)
    soft_state, cache_acc = over_blocks(
        both_rows, ((empty_max, empty_total, empty_sum), empty_cache), portion, key_positions
    )
    running_max, row_total, accum_sum = soft_state
    attended = (
        (accum_sum / row_total[..., None])
        .astype(jnp.bfloat16)
        .reshape(tok_rows, q_local * HEAD_DIM)
    )
    kv_cache = cache_acc.astype(jnp.bfloat16)
    partial_value = jnp.dot(attended, w_out, preferred_element_type=jnp.float32)
    exp_local = w_gate.shape[0]
    experts_all = exp_local * shard_count
    capacity = (tok_rows * TOP * 3 // (2 * experts_all) + 7) // 8 * 8
    flat_ids = expert_ids.reshape(tok_rows * TOP)
    expert_hits = (flat_ids[:, None] == jnp.arange(experts_all, dtype=jnp.int32)[None, :]).astype(
        jnp.int32
    )
    slot_rank = jnp.sum((jnp.cumsum(expert_hits, axis=0) - 1) * expert_hits, axis=1)
    target = flat_ids * capacity + slot_rank
    places = (
        jnp.arange(experts_all * capacity, dtype=jnp.int32)[:, None, None]
        == target.reshape(tok_rows, TOP)[None, :, :]
    )
    selector = jnp.any(places, axis=2).astype(jnp.bfloat16)
    attn_full = lax.psum(partial_value.astype(jnp.bfloat16), "tp").astype(jnp.float32)
    mid = (hidden.astype(jnp.float32) + attn_full).astype(jnp.bfloat16)
    moe_in = rms_norm(mid, gain_moe)
    residual = lax.dynamic_slice_in_dim(mid, tensor_index * quarter, quarter, 1)
    packed = jnp.dot(selector, moe_in, preferred_element_type=jnp.float32).astype(jnp.bfloat16)
    rows_in = lax.all_to_all(
        packed.reshape(shard_count, exp_local, capacity, moe_in.shape[1]),
        "seq",
        split_axis=0,
        concat_axis=0,
        tiled=True,
    )
    gate_term = jnp.einsum("secd,edf->secf", rows_in, w_gate, preferred_element_type=jnp.float32)
    up_term = jnp.einsum("secd,edf->secf", rows_in, w_up, preferred_element_type=jnp.float32)
    hidden_act = (jax.nn.silu(gate_term) * up_term).astype(jnp.bfloat16)
    down_term = jnp.einsum("secf,efd->secd", hidden_act, w_down, preferred_element_type=jnp.float32)
    merged = lax.psum_scatter(down_term.astype(jnp.bfloat16), "tp", scatter_dimension=3, tiled=True)
    returned = lax.all_to_all(merged, "seq", split_axis=0, concat_axis=0, tiled=True)
    flat_back = returned.reshape(experts_all * capacity, quarter)
    picked = jnp.take(flat_back, target, axis=0).astype(jnp.float32).reshape(tok_rows, TOP, quarter)
    moe_out = jnp.einsum("tk,tkd->td", expert_gates, picked)
    final_rows = (residual.astype(jnp.float32) + moe_out).astype(jnp.bfloat16)
    return (final_rows, kv_cache)


def solution(mesh):
    placed = (
        P("seq", None),
        P(),
        P(None, "tp"),
        P(None, "tp"),
        P(None, "tp"),
        P("tp", None),
        P(),
        P("seq", None),
        P("seq", None),
        P("seq", None, "tp"),
        P("seq", None, "tp"),
        P("seq", "tp", None),
        P(),
        P(),
    )
    return jax.shard_map(
        local,
        mesh=mesh,
        in_specs=placed,
        out_specs=(P("seq", "tp"), P("seq", None, "tp")),
        check_vma=False,
    )
```

profile of v0, /device:TPU:1, one launch (start us, length us, event | category | flops | bytes accessed | tf_op | source)
XLA Modules:
  0.0 593.0 jit_solution(5520721394446283536)
XLA Ops:
  7.3 1.5 fusion.47
  11.5 1.7 fusion.55
  13.3 1.7 convolution_bitcast_fusion.1
  17.0 3.6 fusion.80
  23.4 41.2 %all-gather.2.cloned.1.call-done = bf16[4096,1,2,128]{0,3,2,1:T(8,128)(2,1)} async-done(((bf16[128,1,2,128]{0,3,2,1:T(8,128)(2,1)}), bf16[4096,1,2,128]{0,3,2,1:T(8,128)(2,1)}) %all-gather.2.cloned.1.call-update) | async-done | bytes 2097168 | tf_op jit(solution)/shard_map/all_gather | solution.py:178
  64.5 3.8 copy.103
  68.3 4.5 copy.78
  72.9 104.9 %while.17 = (s32[]{:T(128)}, f32[128,1,5]{0,2,1:T(8,128)S(1)}, f32[128,1,5]{0,2,1:T(8,128)S(1)}, f32[128,1,5,128]{0,3,2,1:T(8,128)}, f32[64,16,256]{2,1,0:T(8,12...) while((s32[]{:T(128)}, f32[128,1,5]{0,2,1:T(8,128)S(1)}, ...), condition=%wide.region_6.7_spmd.clone, body=%wide.region_3.6_spmd.clone.sunk | while | flops 440652672 | bytes 13333522 | solution.py:54
  74.9 1.4 compare_and_fusion.3
  79.2 1.8 reshape.490
  81.0 2.5 fusion.113
  87.7 1.4 compare_and_fusion.3
  92.0 1.8 reshape.490
  93.8 2.9 fusion.113
  100.9 1.4 compare_and_fusion.3
  105.1 1.8 reshape.490
  107.0 2.9 fusion.113
  114.0 1.4 compare_and_fusion.3
  118.3 1.8 reshape.490
  120.1 2.9 fusion.113
  131.4 1.8 reshape.490
  133.3 2.9 fusion.113
  144.6 1.8 reshape.490
  146.5 2.9 fusion.113
  157.8 1.8 reshape.490
  159.6 2.9 fusion.113
  170.9 1.8 reshape.490
  172.8 2.9 fusion.113
  178.8 1.6 convolution_convert_fusion.1
  180.6 1.8 reduce-window.20
  183.9 37.5 %all-reduce.2.cloned.1.call-done = bf16[128,2560]{1,0:T(8,128)(2,1)} async-done(((bf16[128,2560]{1,0:T(8,128)(2,1)}), bf16[128,2560]{1,0:T(8,128)(2,1)}) %all-reduce.2.cloned.1.call-update) | async-done | bytes 655376 | tf_op jit(solution)/shard_map/psum | solution.py:205
  221.4 1.4 fusion.44
  222.8 2.3 convolution_convert_fusion
  225.1 99.8 %all_to_all.10 = bf16[32,2,24,2560]{3,2,1,0:T(8,128)(2,1)S(1)} all-to-all(bf16[32,2,24,2560]{3,2,1,0:T(8,128)(2,1)S(1)} %bitcast.173), channel_id=1, replica_groups=mesh['seq'=32,'tp'=4] {'seq'}, dimensions={0} | all-to-all | bytes 15728640 | tf_op jit(solution)/shard_map/all_to_all | solution.py:210
  324.9 3.1 copy-done.6
  328.0 4.4 fusion.26
  332.4 13.8 %convert_bitcast_fusion = bf16[32,2,24,2560]{3,2,0,1:T(8,128)(2,1)} fusion(bf16[2,384,2560]{2,1,0:T(8,128)(2,1)} %param.27, f32[2,32,24,384]{3,2,1,0:T(8,128)S(1)} %fusion.26, bf16[2,2560,384]{2,1,0:T(8,128)(2,1)} %param.26, bf16[32,2,24,2560]{3,2,1,0:T(8,128)(2,1)} %copy-done.6), kind=kOutput, calls=%fused_computation.36 | convolution fusion | flops 6047268864 | bytes 25952256 | tf_op jit(solution)/shard_map/secf,efd->secd/dot_general | solution.py:220
  346.2 35.5 %copy.99 = bf16[32,2,24,2560]{2,0,1,3:T(8,128)(2,1)} copy(bf16[32,2,24,2560]{3,2,0,1:T(8,128)(2,1)} %convert_bitcast_fusion) | data formatting | bytes 15728640
  381.7 57.5 %reshape.481 = bf16[2560,1536]{1,0:T(8,128)(2,1)} reshape(bf16[2560,2,32,24]{3,2,1,0:T(8,128)(2,1)} %bitcast.172) | data formatting | bytes 15728640
  439.3 73.7 %reduce-scatter.4.cloned.1.call-done = bf16[640,1536]{1,0:T(8,128)(2,1)} async-done(((bf16[2560,1536]{1,0:T(8,128)(2,1)}), bf16[640,1536]{1,0:T(8,128)(2,1)}) %reduce-scatter.4.cloned.1.call-update) | async-done | bytes 1966096
  513.0 18.8 %reshape.482 = bf16[640,2,32,24]{3,2,1,0:T(8,128)(2,1)} reshape(bf16[640,1536]{1,0:T(8,128)(2,1)} %reduce-scatter.4.cloned.1.call-done) | data formatting | bytes 3932160
  531.9 10.0 %copy.87 = bf16[32,2,24,640]{3,2,1,0:T(8,128)(2,1)} copy(bf16[32,2,24,640]{2,0,1,3:T(8,128)(2,1)} %bitcast.175) | data formatting | bytes 3932160 | tf_op jit(solution)/shard_map/reduce_scatter | solution.py:221
  541.9 7.7 %all-to-all-start.1 = ((bf16[32,2,24,640]{3,2,1,0:T(8,128)(2,1)}), bf16[32,2,24,640]{3,2,1,0:T(8,128)(2,1)S(1)}, u32[]{:S(2)}, u32[]{:S(2)}) async-start(bf16[32,2,24,640]{3,2,1,0:T(8,128)(2,1)} %copy.87), calls=%async_computation.1 | async-start | bytes 3932160 | tf_op jit(solution)/shard_map/all_to_all | solution.py:222
  551.1 25.4 %all-to-all-done.1 = bf16[32,2,24,640]{3,2,1,0:T(8,128)(2,1)S(1)} async-done(((bf16[32,2,24,640]{3,2,1,0:T(8,128)(2,1)}), bf16[32,2,24,640]{3,2,1,0:T(8,128)(2,1)S(1)}, u32[]{:S(2)}, u32[]{:S(2)}) %all-to-all-start.1) | async-done | bytes 1966112 | tf_op jit(solution)/shard_map/all_to_all | solution.py:222
  576.5 3.4 gather_fusion
  580.0 2.9 gather.7
  582.9 1.9 fusion.51
  584.8 1.6 fusion.60
  (239 shorter events, 73.2 us)
Async XLA Ops:
  7.2 171.6 %copy-start = (bf16[640,2560]{1,0:T(8,128)(2,1)S(1)}, bf16[640,2560]{1,0:T(8,128)(2,1)}, u32[]{:S(2)}) copy-start(bf16[640,2560]{1,0:T(8,128)(2,1)} %param.21) | copy-start | bytes 9830404
  7.2 6.1 %copy-start.14 = (f32[2560]{0:T(1024)S(1)}, f32[2560]{0:T(1024)}, u32[]{:S(2)}) copy-start(f32[2560]{0:T(1024)} %param.17) | copy-start | bytes 30724
  7.2 8.8 %copy-start.12 = (s32[128,6]{0,1:T(8,128)S(1)}, s32[128,6]{0,1:T(8,128)}, u32[]{:S(2)}) copy-start(s32[128,6]{0,1:T(8,128)} %param.23) | copy-start | bytes 9220
  7.2 57.3 %all-gather.2.cloned.1.call-start = ((), (), s32[]{:S(2)}) async-start(), calls=%async_computation.3 | async-start | bytes 2162688 | tf_op jit(solution)/shard_map/all_gather | solution.py:178
  15.9 205.5 %all-reduce.2.cloned.1.call-start = ((), (), s32[]{:S(2)}) async-start(), calls=%async_computation.4 | async-start | bytes 1310720 | tf_op jit(solution)/shard_map/psum | solution.py:205
  16.1 4.5 copy-start.10
  81.0 2.5 copy-start.3
  81.0 2.5 copy-start.7
  83.6 1.0 copy-start.4
  84.9 0.7 copy-start.5
  93.8 2.9 copy-start.3
  93.8 2.9 copy-start.7
  96.7 1.0 copy-start.4
  98.1 0.7 copy-start.5
  107.0 2.9 copy-start.3
  107.0 2.9 copy-start.7
  109.9 1.0 copy-start.4
  111.3 0.7 copy-start.5
  120.1 2.9 copy-start.3
  120.1 2.9 copy-start.7
  123.0 1.0 copy-start.4
  124.4 0.7 copy-start.5
  133.3 2.9 copy-start.3
  133.3 2.9 copy-start.7
  136.2 1.0 copy-start.4
  137.6 0.7 copy-start.5
  146.4 2.9 copy-start.3
  146.4 2.9 copy-start.7
  149.4 1.0 copy-start.4
  150.7 0.7 copy-start.5
  159.6 2.9 copy-start.3
  159.6 2.9 copy-start.7
  162.5 1.0 copy-start.4
  172.8 2.9 copy-start.3
  172.8 2.9 copy-start.7
  175.7 1.0 copy-start.4
  178.8 1.7 copy-start.13
  178.8 1.7 copy-start.11
  180.4 41.0 %copy-start.8 = (bf16[128,2560]{1,0:T(8,128)(2,1)S(1)}, bf16[128,2560]{1,0:T(8,128)(2,1)}, u32[]{:S(2)}) copy-start(bf16[128,2560]{1,0:T(8,128)(2,1)} %param.16) | copy-start | bytes 1966084
  180.4 42.4 %copy-start.15 = (f32[2560]{0:T(1024)S(1)}, f32[2560]{0:T(1024)}, u32[]{:S(2)}) copy-start(f32[2560]{0:T(1024)} %param.22) | copy-start | bytes 30724
  180.4 332.6 %reduce-scatter.4.cloned.1.call-start = ((), (), s32[]{:S(2)}) async-start(), calls=%async_computation.5 | async-start | bytes 9830400
  222.8 2.3 copy-start.9
  225.1 102.8 %copy-start.17 = (bf16[2,2560,384]{2,1,0:T(8,128)(2,1)S(1)}, bf16[2,2560,384]{2,1,0:T(8,128)(2,1)}, u32[]{:S(2)}) copy-start(bf16[2,2560,384]{2,1,0:T(8,128)(2,1)} %param.25) | copy-start | bytes 11796484
  324.9 3.1 copy-start.6
  541.9 8.0 %copy-start.16 = (f32[128,6]{0,1:T(8,128)S(1)}, f32[128,6]{0,1:T(8,128)}, u32[]{:S(2)}) copy-start(f32[128,6]{0,1:T(8,128)} %param.24) | copy-start | bytes 9220
  541.9 8.4 %copy-start.2 = (f32[64,16,256]{2,1,0:T(8,128)S(1)}, f32[64,16,256]{2,1,0:T(8,128)}, u32[]{:S(2)}) copy-start(f32[64,16,256]{2,1,0:T(8,128)} %get-tuple-element.63) | copy-start | bytes 3145732
  541.9 34.6 %all-to-all-start.1 = ((bf16[32,2,24,640]{3,2,1,0:T(8,128)(2,1)}), bf16[32,2,24,640]{3,2,1,0:T(8,128)(2,1)S(1)}, u32[]{:S(2)}, u32[]{:S(2)}) async-start(bf16[32,2,24,640]{3,2,1,0:T(8,128)(2,1)} %copy.87), calls=%async_computation.1 | async-start | bytes 3932160 | tf_op jit(solution)/shard_map/all_to_all | solution.py:222
  580.0 6.5 %copy-start.1 = (bf16[640,2560]{1,0:T(8,128)(2,1)S(1)}, bf16[640,2560]{1,0:T(8,128)(2,1)}, u32[]{:S(2)}) copy-start(bf16[640,2560]{1,0:T(8,128)(2,1)} %param.21) | copy-start | bytes 9830404
  (2 other events, 1.5 us)
Sparse Core Ops, SparseCore 0:
  16.0 48.5 all-gather.1
  180.5 40.8 all-reduce.1
  439.4 73.5 reduce-scatter.3
where the time goes:
time: 598 us; the launch traced here: 593 us
  local copies, waits for them, and re-layouts  195 us (33%)
  waiting for transfers between devices  178 us (30%)
  blocking collectives  99.8 us (17%)
  matrix products  59.8 us (10%)
  other arithmetic  37.6 us (6%)
  between operations  14.1 us (2%)
  starting transfers between devices  7.86 us (1%)
    unnamed x36, local copies, waits for them, and re-layouts  124 us
    all_to_all x1, blocking collectives, local(): lax.all_to_all(packed.reshape(shard_count, exp_local, capacity, moe_in.sh...  99.8 us
    unnamed x4, waiting for transfers between devices  73.8 us
    all_gather x1, waiting for transfers between devices, local(): portion = lax.all_gather(kv_rows, 'seq', axis=0, tiled=True)  41.2 us
    psum x1, waiting for transfers between devices, local(): lax.psum(partial_value.astype(jnp.bfloat16), 'tp').astype(jnp.float32)  37.5 us
    all_to_all x1, waiting for transfers between devices, local(): lax.all_to_all(merged, 'seq', split_axis=0, concat_axis=0, tiled=True)  25.4 us
    dot_general x8, matrix products, cache_rows(): jnp.einsum('spc,cw->spw', chosen, portion.reshape(piece_rows, row_width),...  22.8 us
    dynamic_slice x24, local copies, waits for them, and re-layouts, over_blocks(): carried, unused = lax.scan(turn, carried, (stacked, pos_stack))  21.4 us
  transfers between devices with their start and end apart: 4, of which 4 were waited for; matrix products, arithmetic and copies ran while one was open for 2% of the time, Pallas kernels for 0%

commit v1 on v0

--- a/solution.py
+++ b/solution.py
@@ -175,7 +175,9 @@
             cache_rows(cache_acc, portion, key_positions),
         )
 
-    portion = lax.all_gather(kv_rows, "seq", axis=0, tiled=True)
+    portion = jnp.concatenate(
+        lax.all_to_all(jnp.stack([kv_rows] * lax.axis_size("seq")), "seq", 0, 0), axis=0
+    )
     key_positions = jnp.arange(portion.shape[0], dtype=jnp.int32)
     soft_state, cache_acc = over_blocks(
         both_rows, ((empty_max, empty_total, empty_sum), empty_cache), portion, key_positions

time: 598 us -> 557 us (0.931)
  waiting for transfers between devices: 178 us -> 157 us
  local copies, waits for them, and re-layouts: 195 us -> 179 us
  other arithmetic: 37.6 us -> 24.9 us
  starting transfers between devices: 7.86 us -> 17.4 us
    all_gather x1 -> x0, waiting for transfers between devices: 41.2 us -> none  [local(): portion = lax.all_gather(kv_rows, 'seq', axis=0, tiled=True)]
    all_to_all x0 -> x1, waiting for transfers between devices: none -> 22 us  [local(): lax.all_to_all(jnp.stack([kv_rows] * lax.axis_size('seq')), 'seq', 0, 0)]
    all_to_all x0 -> x1, starting transfers between devices: none -> 9.61 us  [local(): lax.all_to_all(jnp.stack([kv_rows] * lax.axis_size('seq')), 'seq', 0, 0)]
    unnamed x36 -> x34, local copies, waits for them, and re-layouts: 124 us -> 116 us
    squeeze x8 -> x0, local copies, waits for them, and re-layouts: 7.74 us -> none  [over_blocks(): carried, unused = lax.scan(turn, carried, (stacked, pos_stack))]
    unnamed x4 -> x3, waiting for transfers between devices: 73.8 us -> 73.8 us
where the time goes in v1:
time: 557 us; the launch traced here: 554 us
  local copies, waits for them, and re-layouts  179 us (32%)
  waiting for transfers between devices  157 us (28%)
  blocking collectives  99.8 us (18%)
  matrix products  59.2 us (11%)
  other arithmetic  24.9 us (4%)
  starting transfers between devices  17.4 us (3%)
  between operations  14.4 us (3%)
    unnamed x34, local copies, waits for them, and re-layouts  116 us
    all_to_all x1, blocking collectives, local(): lax.all_to_all(packed.reshape(shard_count, exp_local, capacity, moe_in.sh...  99.8 us
    unnamed x3, waiting for transfers between devices  73.8 us
    psum x1, waiting for transfers between devices, local(): lax.psum(partial_value.astype(jnp.bfloat16), 'tp').astype(jnp.float32)  36.2 us
    all_to_all x1, waiting for transfers between devices, local(): lax.all_to_all(merged, 'seq', split_axis=0, concat_axis=0, tiled=True)  25.4 us
    dot_general x8, matrix products, cache_rows(): jnp.einsum('spc,cw->spw', chosen, portion.reshape(piece_rows, row_width),...  22.2 us
    all_to_all x1, waiting for transfers between devices, local(): lax.all_to_all(jnp.stack([kv_rows] * lax.axis_size('seq')), 'seq', 0, 0)  22 us
    dynamic_slice x24, local copies, waits for them, and re-layouts, over_blocks(): carried, unused = lax.scan(turn, carried, (stacked, pos_stack))  21.8 us
  transfers between devices with their start and end apart: 4, of which 4 were waited for; matrix products, arithmetic and copies ran while one was open for 2% of the time, Pallas kernels for 0%

profile of v1, /device:TPU:1, one launch (start us, length us, event | category | flops | bytes accessed | tf_op | source)
XLA Modules:
  0.0 553.5 jit_solution(6956202927745606)
XLA Ops:
  7.2 1.5 fusion.47
  10.3 1.7 fusion.55
  12.1 1.7 convolution_bitcast_fusion.1
  14.2 1.9 stack.8
  16.1 9.6 %all-to-all-start = ((bf16[32,128,1,2,128]{4,1,3,2,0:T(8,128)(2,1)}), bf16[32,128,1,2,128]{4,1,3,2,0:T(8,128)(2,1)}, u32[]{:S(2)}, u32[]{:S(2)}) async-start(bf16[32,128,1,2,128]{4,1,3,2,0:T(8,128)(2,1)} %stack.8), calls=%async_computation | async-start | bytes 4194304 | tf_op jit(solution)/shard_map/all_to_all | solution.py:179
  26.8 3.6 fusion.80
  32.0 22.0 %all-to-all-done = bf16[32,128,1,2,128]{4,1,3,2,0:T(8,128)(2,1)} async-done(((bf16[32,128,1,2,128]{4,1,3,2,0:T(8,128)(2,1)}), bf16[32,128,1,2,128]{4,1,3,2,0:T(8,128)(2,1)}, u32[]{:S(2)}, u32[]{:S(2)}) %all-to-all-start) | async-done | bytes 2097184 | tf_op jit(solution)/shard_map/all_to_all | solution.py:179
  54.0 3.2 copy.83
  57.2 82.0 %while.17 = (s32[]{:T(128)}, f32[128,1,5]{0,2,1:T(8,128)S(1)}, f32[128,1,5]{0,2,1:T(8,128)S(1)}, f32[128,1,5,128]{0,3,2,1:T(8,128)}, f32[64,16,256]{2,1,0:T(8,12...) while((s32[]{:T(128)}, f32[128,1,5]{0,2,1:T(8,128)S(1)}, ...), condition=%wide.region_6.7_spmd.clone, body=%wide.region_3.6_spmd.clone.sunk | while | flops 440652672 | bytes 14257362 | solution.py:54
  58.7 1.7 dynamic-slice_bitcast_fusion.3
  62.5 2.3 fusion.110
  68.5 1.7 dynamic-slice_bitcast_fusion.3
  72.4 2.8 fusion.110
  78.8 1.7 dynamic-slice_bitcast_fusion.3
  82.7 2.8 fusion.110
  89.1 1.7 dynamic-slice_bitcast_fusion.3
  91.9 1.1 reshape.489
  93.0 2.8 fusion.110
  99.5 1.7 dynamic-slice_bitcast_fusion.3
  102.2 1.1 reshape.489
  103.3 2.8 fusion.110
  109.8 1.7 dynamic-slice_bitcast_fusion.3
  112.5 1.1 reshape.489
  113.7 2.8 fusion.110
  120.1 1.7 dynamic-slice_bitcast_fusion.3
  124.0 2.8 fusion.110
  130.4 1.7 dynamic-slice_bitcast_fusion.3
  134.3 2.8 fusion.110
  140.3 1.6 convolution_convert_fusion.1
  142.1 1.8 reduce-window.20
  145.4 36.2 %all-reduce.2.cloned.1.call-done = bf16[128,2560]{1,0:T(8,128)(2,1)} async-done(((bf16[128,2560]{1,0:T(8,128)(2,1)}), bf16[128,2560]{1,0:T(8,128)(2,1)}) %all-reduce.2.cloned.1.call-update) | async-done | bytes 655376 | tf_op jit(solution)/shard_map/psum | solution.py:207
  181.6 1.4 fusion.44
  183.0 2.3 convolution_convert_fusion
  185.3 99.8 %all_to_all.15 = bf16[32,2,24,2560]{3,2,1,0:T(8,128)(2,1)S(1)} all-to-all(bf16[32,2,24,2560]{3,2,1,0:T(8,128)(2,1)S(1)} %bitcast.172), channel_id=1, replica_groups=mesh['seq'=32,'tp'=4] {'seq'}, dimensions={0} | all-to-all | bytes 15728640 | tf_op jit(solution)/shard_map/all_to_all | solution.py:212
  285.1 3.1 copy-done.7
  288.2 4.4 fusion.26
  292.6 13.8 %convert_bitcast_fusion = bf16[32,2,24,2560]{3,2,0,1:T(8,128)(2,1)} fusion(bf16[2,384,2560]{2,1,0:T(8,128)(2,1)} %param.27, f32[2,32,24,384]{3,2,1,0:T(8,128)S(1)} %fusion.26, bf16[2,2560,384]{2,1,0:T(8,128)(2,1)} %param.26, bf16[32,2,24,2560]{3,2,1,0:T(8,128)(2,1)} %copy-done.7), kind=kOutput, calls=%fused_computation.37 | convolution fusion | flops 6047268864 | bytes 25952256 | tf_op jit(solution)/shard_map/secf,efd->secd/dot_general | solution.py:222
  306.4 35.5 %copy.106 = bf16[32,2,24,2560]{2,0,1,3:T(8,128)(2,1)} copy(bf16[32,2,24,2560]{3,2,0,1:T(8,128)(2,1)} %convert_bitcast_fusion) | data formatting | bytes 15728640
  342.0 57.5 %reshape.480 = bf16[2560,1536]{1,0:T(8,128)(2,1)} reshape(bf16[2560,2,32,24]{3,2,1,0:T(8,128)(2,1)} %bitcast.171) | data formatting | bytes 15728640
  399.5 73.7 %reduce-scatter.4.cloned.1.call-done = bf16[640,1536]{1,0:T(8,128)(2,1)} async-done(((bf16[2560,1536]{1,0:T(8,128)(2,1)}), bf16[640,1536]{1,0:T(8,128)(2,1)}) %reduce-scatter.4.cloned.1.call-update) | async-done | bytes 1966096
  473.2 18.8 %reshape.481 = bf16[640,2,32,24]{3,2,1,0:T(8,128)(2,1)} reshape(bf16[640,1536]{1,0:T(8,128)(2,1)} %reduce-scatter.4.cloned.1.call-done) | data formatting | bytes 3932160
  492.1 10.0 %copy.94 = bf16[32,2,24,640]{3,2,1,0:T(8,128)(2,1)} copy(bf16[32,2,24,640]{2,0,1,3:T(8,128)(2,1)} %bitcast.174) | data formatting | bytes 3932160 | tf_op jit(solution)/shard_map/reduce_scatter | solution.py:223
  502.1 7.7 %all-to-all-start.2 = ((bf16[32,2,24,640]{3,2,1,0:T(8,128)(2,1)}), bf16[32,2,24,640]{3,2,1,0:T(8,128)(2,1)S(1)}, u32[]{:S(2)}, u32[]{:S(2)}) async-start(bf16[32,2,24,640]{3,2,1,0:T(8,128)(2,1)} %copy.94), calls=%async_computation.2 | async-start | bytes 3932160 | tf_op jit(solution)/shard_map/all_to_all | solution.py:224
  511.4 25.4 %all-to-all-done.2 = bf16[32,2,24,640]{3,2,1,0:T(8,128)(2,1)S(1)} async-done(((bf16[32,2,24,640]{3,2,1,0:T(8,128)(2,1)}), bf16[32,2,24,640]{3,2,1,0:T(8,128)(2,1)S(1)}, u32[]{:S(2)}, u32[]{:S(2)}) %all-to-all-start.2) | async-done | bytes 1966112 | tf_op jit(solution)/shard_map/all_to_all | solution.py:224
  536.8 3.4 gather_fusion
  540.2 2.9 gather.7
  543.1 1.9 fusion.51
  545.0 1.6 fusion.60
  (343 shorter events, 50.2 us)
Async XLA Ops:
  7.2 133.1 %copy-start = (bf16[640,2560]{1,0:T(8,128)(2,1)S(1)}, bf16[640,2560]{1,0:T(8,128)(2,1)}, u32[]{:S(2)}) copy-start(bf16[640,2560]{1,0:T(8,128)(2,1)} %param.21) | copy-start | bytes 9830404
  7.2 4.9 copy-start.21
  16.1 9.7 %copy-start.15 = (s32[128,6]{0,1:T(8,128)S(1)}, s32[128,6]{0,1:T(8,128)}, u32[]{:S(2)}) copy-start(s32[128,6]{0,1:T(8,128)} %param.23) | copy-start | bytes 9220
  16.1 38.0 %all-to-all-start = ((bf16[32,128,1,2,128]{4,1,3,2,0:T(8,128)(2,1)}), bf16[32,128,1,2,128]{4,1,3,2,0:T(8,128)(2,1)}, u32[]{:S(2)}, u32[]{:S(2)}) async-start(bf16[32,128,1,2,128]{4,1,3,2,0:T(8,128)(2,1)} %stack.8), calls=%async_computation | async-start | bytes 4194304 | tf_op jit(solution)/shard_map/all_to_all | solution.py:179
  25.7 155.9 %all-reduce.2.cloned.1.call-start = ((), (), s32[]{:S(2)}) async-start(), calls=%async_computation.4 | async-start | bytes 1310720 | tf_op jit(solution)/shard_map/psum | solution.py:207
  25.9 4.5 copy-start.11
  57.2 3.2 copy-start.13
  57.2 3.2 copy-start.17
  57.2 3.2 copy-start.19
  67.0 3.2 copy-start.13
  67.0 3.2 copy-start.17
  67.0 3.2 copy-start.19
  72.4 2.9 copy-start.3
  72.4 2.9 copy-start.4
  77.3 3.2 copy-start.13
  77.3 3.2 copy-start.17
  77.4 3.2 copy-start.19
  82.7 2.9 copy-start.3
  87.7 3.2 copy-start.13
  87.7 3.2 copy-start.17
  87.7 3.2 copy-start.19
  93.0 2.9 copy-start.3
  93.0 2.9 copy-start.4
  98.0 3.2 copy-start.13
  98.0 3.2 copy-start.17
  98.0 3.2 copy-start.19
  103.3 2.9 copy-start.3
  108.3 3.2 copy-start.13
  108.3 3.2 copy-start.17
  108.3 3.2 copy-start.19
  113.6 2.9 copy-start.3
  118.6 3.2 copy-start.13
  118.6 3.2 copy-start.17
  118.6 3.2 copy-start.19
  124.0 2.9 copy-start.3
  128.9 3.2 copy-start.13
  128.9 3.2 copy-start.17
  129.0 3.2 copy-start.19
  134.3 2.9 copy-start.3
  141.9 39.7 %copy-start.9 = (bf16[128,2560]{1,0:T(8,128)(2,1)S(1)}, bf16[128,2560]{1,0:T(8,128)(2,1)}, u32[]{:S(2)}) copy-start(bf16[128,2560]{1,0:T(8,128)(2,1)} %param.16) | copy-start | bytes 1966084
  141.9 41.2 %copy-start.22 = (f32[2560]{0:T(1024)S(1)}, f32[2560]{0:T(1024)}, u32[]{:S(2)}) copy-start(f32[2560]{0:T(1024)} %param.22) | copy-start | bytes 30724
  141.9 331.4 %reduce-scatter.4.cloned.1.call-start = ((), (), s32[]{:S(2)}) async-start(), calls=%async_computation.5 | async-start | bytes 9830400
  185.3 102.8 %copy-start.24 = (bf16[2,2560,384]{2,1,0:T(8,128)(2,1)S(1)}, bf16[2,2560,384]{2,1,0:T(8,128)(2,1)}, u32[]{:S(2)}) copy-start(bf16[2,2560,384]{2,1,0:T(8,128)(2,1)} %param.25) | copy-start | bytes 11796484
  285.1 3.1 copy-start.7
  502.1 8.0 %copy-start.23 = (f32[128,6]{0,1:T(8,128)S(1)}, f32[128,6]{0,1:T(8,128)}, u32[]{:S(2)}) copy-start(f32[128,6]{0,1:T(8,128)} %param.24) | copy-start | bytes 9220
  502.1 8.4 %copy-start.2 = (f32[64,16,256]{2,1,0:T(8,128)S(1)}, f32[64,16,256]{2,1,0:T(8,128)}, u32[]{:S(2)}) copy-start(f32[64,16,256]{2,1,0:T(8,128)} %get-tuple-element.63) | copy-start | bytes 3145732
  502.1 34.6 %all-to-all-start.2 = ((bf16[32,2,24,640]{3,2,1,0:T(8,128)(2,1)}), bf16[32,2,24,640]{3,2,1,0:T(8,128)(2,1)S(1)}, u32[]{:S(2)}, u32[]{:S(2)}) async-start(bf16[32,2,24,640]{3,2,1,0:T(8,128)(2,1)} %copy.94), calls=%async_computation.2 | async-start | bytes 3932160 | tf_op jit(solution)/shard_map/all_to_all | solution.py:224
  540.2 6.5 %copy-start.1 = (bf16[640,2560]{1,0:T(8,128)(2,1)S(1)}, bf16[640,2560]{1,0:T(8,128)(2,1)}, u32[]{:S(2)}) copy-start(bf16[640,2560]{1,0:T(8,128)(2,1)} %param.21) | copy-start | bytes 9830404
  (58 other events, 102.1 us)
Sparse Core Ops, SparseCore 0:
  142.0 39.5 all-reduce.1
  399.6 73.5 reduce-scatter.3
